TPU v7x, 32 devices: a whole 2x2x4 slice. The times are simulated.
32 devices in a mesh: snap: 4 (over z), vert: 8 (over y, x, core).
Axes of the slice: x: 2, y: 2, z: 4, core: 2. Of those that a mesh axis runs over, the one named last changes fastest.
Arguments:
- features: bfloat16 [4, 6144, 128], P('snap', 'vert'), may hold values from -6 to 6
- adjacency_tiles: bfloat16 [4, 96, 128, 128], P('snap', 'vert'), may hold values from -0.375 to 0.375
- src_block: int32 [4, 96], P('snap', 'vert'), may hold values from 0 to 47, as said below
- dst_block: int32 [4, 96], P('snap', 'vert'), may hold values from 0 to 5
- block_count: int32 [4, 8], P('snap', 'vert'), may hold values from 6 to 12, as said below
- w_conv: bfloat16 [128, 512], replicated, may hold values from -0.5 to 0.5
- b_conv: float32 [512], replicated, may hold values from -3 to 3
- w_input: bfloat16 [512, 2048], replicated, may hold values from -0.25 to 0.25
- w_state: bfloat16 [512, 2048], replicated, may hold values from -0.25 to 0.25
- b_gates: float32 [2048], replicated, may hold values from -3 to 3
Outputs:
- hidden_seq: bfloat16 [4, 6144, 512], P('snap', 'vert')
Inputs may be any that keep to these rules, and one draw needn't show every extreme that they name: `src_block`: slot s of owner v names a column block held by owner v - 1, v or v + 1 (clipped to the owners that exist); its first slot names one of owner v - 1 and its second one of owner v + 1 where those exist. `block_count`: in every snapshot some owner has all 12 slots live.
All inputs are finite; a program needn't handle non-finite values.
Results may differ from a plain program's by a relative error of at most 0.0044.
Values may be sent and summed in bfloat16 or wider, within the bound.
No kernel may reach another device: no remote copies, remote signals or barrier semaphores. Data moves between devices by JAX's collectives and lax.ppermute only.
A program may use at most 64 MiB of HBM per device.

v0:
```python
import jax
import jax.numpy as jnp
from jax import lax
from jax.sharding import PartitionSpec as P

forget_bias = 2.0


def padded(cells, sides, width):
    for axis, dim in sides:
        count = lax.axis_size(axis)
        ends = count - 1
        head = lax.slice_in_dim(cells, 0, width, axis=dim)
        tail = lax.slice_in_dim(cells, cells.shape[dim] - width, cells.shape[dim], axis=dim)
        cells = jnp.concatenate(
            [
                lax.ppermute(tail, axis, [(i, (i + 1) % count) for i in range(ends)]),
                cells,
                lax.ppermute(head, axis, [((i + 1) % count, i) for i in range(ends)]),
            ],
            axis=dim,
        )
    return cells


def gate_step(hidden, cell, pre_gates, w_state, b_gates):
    width = w_state.shape[0]
    gates = pre_gates + jnp.dot(hidden, w_state, preferred_element_type=jnp.float32) + b_gates
    input_gate = jax.nn.sigmoid(gates[:, :width])
    forget_gate = jax.nn.sigmoid(gates[:, width : 2 * width] + forget_bias)
    candidate = jnp.tanh(gates[:, 2 * width : 3 * width])
    output_gate = jax.nn.sigmoid(gates[:, 3 * width :])
    new_cell = forget_gate * cell + input_gate * candidate
    new_hidden = (output_gate * jnp.tanh(new_cell)).astype(jnp.bfloat16)
    return (new_hidden, new_cell)


def shards(
    features,
    adjacency_tiles,
    src_block,
    dst_block,
    block_count,
    w_conv,
    b_conv,
    w_input,
    w_state,
    b_gates,
):
    vert_rows = features.shape[1]
    feat_width = features.shape[2]
    block_rows = adjacency_tiles.shape[2]
    slot_count = adjacency_tiles.shape[1]
    row_blocks = vert_rows // block_rows
    hid_width = w_state.shape[0]
    owner_index = lax.axis_index("vert")
    window = padded(features, (("vert", 1),), vert_rows)
    window_blocks = window[0].reshape(3 * row_blocks, block_rows, feat_width)
    local_index = src_block[0] - (owner_index - 1) * row_blocks
    picked = jnp.take(window_blocks, local_index, axis=0)
    product = jnp.einsum(
        "ebk,ekf->ebf", adjacency_tiles[0], picked, preferred_element_type=jnp.float32
    )
    alive = jnp.arange(slot_count, dtype=jnp.int32) < block_count[0, 0]
    selector = (
        (dst_block[0][None, :] == jnp.arange(row_blocks, dtype=jnp.int32)[:, None]) & alive[None, :]
    ).astype(jnp.float32)
    summed = jnp.einsum("re,ebf->rbf", selector, product, precision=lax.Precision.HIGHEST)
    summed = summed.reshape(vert_rows, feat_width).astype(jnp.bfloat16)
    conv = jax.nn.relu(jnp.dot(summed, w_conv, preferred_element_type=jnp.float32) + b_conv).astype(
        jnp.bfloat16
    )
    regrouped = lax.all_to_all(conv[None], "snap", split_axis=1, concat_axis=0, tiled=True)
    pre_all = jnp.einsum("tvp,pg->tvg", regrouped, w_input, preferred_element_type=jnp.float32)
    slice_rows = regrouped.shape[1]

    def advance(carry, pre_now):
        hidden, cell = carry
        new_hidden, new_cell = gate_step(hidden, cell, pre_now, w_state, b_gates)
        return ((new_hidden, new_cell), new_hidden)

    start_state = (
        jnp.zeros((slice_rows, hid_width), jnp.bfloat16),
        jnp.zeros((slice_rows, hid_width), jnp.float32),
    )
    _, sequence = lax.scan(advance, start_state, pre_all)
    return lax.all_to_all(sequence, "snap", split_axis=0, concat_axis=1, tiled=True)


def solution(mesh):
    placed = (
        P("snap", "vert", None),
        P("snap", "vert", None, None),
        P("snap", "vert"),
        P("snap", "vert"),
        P("snap", "vert"),
        P(),
        P(),
        P(),
        P(),
        P(),
    )
    return jax.shard_map(
        shards, mesh=mesh, in_specs=placed, out_specs=P("snap", "vert", None), check_vma=False
    )
```

profile of v0, /device:TPU:4, one launch (start us, length us, event | category | flops | bytes accessed | tf_op | source)
XLA Modules:
  0.0 96.3 jit_solution(7456984444435545295)
XLA Ops:
  0.0 2.0 %collective-permute-start = (bf16[1,768,128]{2,1,0:T(8,128)(2,1)}, bf16[1,768,128]{2,1,0:T(8,128)(2,1)S(1)}, u32[]{:S(2)}, u32[]{:S(2)}) collective-permute-start(bf16[1,768,128]{2,1,0:T(8,128)(2,1)} %param.12), channel_id=1, source_target_pairs={{0,1},{1,2},{2,3},{3,4},{4,5},{5,6},{6,7},{8,9},{9,10},{10,11},{11... | collective-permute-start | bytes 589832 | tf_op jit(solution)/shard_map/ppermute | solution.py:17
  2.1 4.5 %collective-permute-start.1 = (bf16[1,768,128]{2,1,0:T(8,128)(2,1)}, bf16[1,768,128]{2,1,0:T(8,128)(2,1)S(1)}, u32[]{:S(2)}, u32[]{:S(2)}) collective-permute-start(bf16[1,768,128]{2,1,0:T(8,128)(2,1)} %param.12), channel_id=1, source_target_pairs={{1,0},{2,1},{3,2},{4,3},{5,4},{6,5},{7,6},{9,8},{10,9},{11,10},{12... | collective-permute-start | bytes 589832 | tf_op jit(solution)/shard_map/ppermute | solution.py:19
  6.6 0.7 fusion.32
  7.9 0.7 compare_and_fusion
  8.6 1.5 %collective-permute-done.1 = bf16[1,768,128]{2,1,0:T(8,128)(2,1)S(1)} collective-permute-done((bf16[1,768,128]{2,1,0:T(8,128)(2,1)}, bf16[1,768,128]{2,1,0:T(8,128)(2,1)S(1)}, u32[]{:S(2)}, u32[]{:S(2)}) %collective-permute-start.1) | collective-permute-done | bytes 196640 | tf_op jit(solution)/shard_map/ppermute | solution.py:19
  10.1 1.0 %pad_maximum_fusion = bf16[1,2304,128]{2,1,0:T(8,128)(2,1)S(1)} fusion(bf16[1,768,128]{2,1,0:T(8,128)(2,1)S(1)} %collective-permute-done.1, bf16[1,768,128]{2,1,0:T(8,128)(2,1)} %param.12, bf16[1,768,128]{2,1,0:T(8,128)(2,1)S(1)} %collective-permute-done), kind=kLoop, calls=%fused_computation.33 | loop fusion | flops 1769472 | bytes 1179648 | tf_op jit(solution)/shard_map/concatenate | solution.py:15
  11.1 0.6 gather_fusion
  11.7 1.4 %convolution_bitcast_fusion = f32[12,128,128]{1,2,0:T(8,128)} fusion(bf16[1,12,128,128]{3,2,1,0:T(8,128)(2,1)S(1)} %copy-done.2, bf16[12,128,128]{2,1,0:T(8,128)(2,1)S(1)} %gather_fusion, pred[12]{0:T(512)(128)(4,1)S(1)} %compare_and_fusion), kind=kOutput, calls=%fused_computation.31 | convolution fusion | flops 50528256 | bytes 1572876 | tf_op jit(solution)/shard_map/ebk,ekf->ebf/dot_general | solution.py:61
  13.1 1.7 %copy.16 = f32[12,128,128]{2,0,1:T(8,128)S(1)} copy(f32[12,128,128]{1,2,0:T(8,128)} %convolution_bitcast_fusion) | data formatting | bytes 1572864 | tf_op jit(solution)/shard_map/ebk,ekf->ebf/dot_general | solution.py:61
  15.7 2.4 %copy.22 = bf16[1,768,512]{2,0,1:T(2,128)(2,1)} copy(bf16[1,768,512]{2,1,0:T(8,128)(2,1)S(1)} %fusion.22) | data formatting | bytes 1572864 | tf_op jit(solution)/shard_map/broadcast_in_dim | solution.py:73
  18.6 6.4 %reduce = bf16[768,512]{1,0:T(8,128)(2,1)S(1)} reduce(bf16[768,1,512]{2,1,0:T(2,128)(2,1)} %bitcast.45, bf16[]{:T(256)} %broadcast.89), dimensions={1}, to_apply=%bitcast.37.reduce_sub_computation | reduce | bytes 1572866
  25.0 1.4 %reshape.53 = bf16[4,2,49152]{2,1,0:T(2,128)(2,1)} reshape(bf16[768,512]{1,0:T(8,128)(2,1)S(1)} %reduce) | data formatting | bytes 1572864
  26.4 4.9 %all-to-all-start = ((bf16[4,2,49152]{2,1,0:T(2,128)(2,1)}), bf16[4,2,49152]{2,1,0:T(2,128)(2,1)S(1)}, u32[]{:S(2)}, u32[]{:S(2)}) async-start(bf16[4,2,49152]{2,1,0:T(2,128)(2,1)} %reshape.53), calls=%async_computation | async-start | bytes 1572864 | tf_op jit(solution)/shard_map/all_to_all | solution.py:73
  31.3 21.0 %all-to-all-done = bf16[4,2,49152]{2,1,0:T(2,128)(2,1)S(1)} async-done(((bf16[4,2,49152]{2,1,0:T(2,128)(2,1)}), bf16[4,2,49152]{2,1,0:T(2,128)(2,1)S(1)}, u32[]{:S(2)}, u32[]{:S(2)}) %all-to-all-start) | async-done | bytes 786464 | tf_op jit(solution)/shard_map/all_to_all | solution.py:73
  52.3 2.1 %reshape.54 = bf16[768,1,512]{2,1,0:T(2,128)(2,1)} reshape(bf16[4,2,49152]{2,1,0:T(2,128)(2,1)S(1)} %all-to-all-done) | data formatting | bytes 1572864
  54.4 1.6 %copy.20 = bf16[1,768,512]{2,1,0:T(8,128)(2,1)S(1)} copy(bf16[1,768,512]{2,0,1:T(2,128)(2,1)} %bitcast.46) | data formatting | bytes 1572864
  56.0 4.5 %fusion.20 = f32[4,192,2048]{2,1,0:T(8,128)} fusion(bf16[4,192,512]{2,1,0:T(8,128)(2,1)S(1)} %bitcast.47, bf16[512,2048]{1,0:T(8,128)(2,1)S(1)} %copy-done), kind=kOutput, calls=%fused_computation.27 | convolution fusion | flops 1610612736 | bytes 9175040 | tf_op jit(solution)/shard_map/tvp,pg->tvg/dot_general | solution.py:74
  60.5 12.3 %while.15 = (s32[]{:T(128)}, bf16[192,512]{1,0:T(8,128)(2,1)S(1)}, f32[192,512]{1,0:T(8,128)S(1)}, bf16[4,192,512]{2,1,0:T(8,128)(2,1)S(1)}, f32[4,192,2048]{2,1...) while((s32[]{:T(128)}, bf16[192,512]{1,0:T(8,128)(2,1)S(1)}, ...), condition=%wide.region_1.2_spmd.clone, body=%wide.region_0.1_spmd.clone.sunk | while | flops 405110784 | bytes 8200304 | solution.py:86
  60.5 2.6 %fusion.46 = f32[192,2048]{1,0:T(8,128)S(1)} fusion(bf16[512,2048]{1,0:T(8,128)(2,1)} %get-tuple-element.156, f32[4,192,2048]{2,1,0:T(8,128)} %get-tuple-element.155, s32[]{:T(128)} %get-tuple-element.142, f32[2048]{0:T(1024)S(1)} %get-tuple-element.157, bf16[192,512]{1,0:T(8,128)(2,1)S(1)} %get-tuple-element.143, pred[]{:T(512)S(6)} %compare.3), kind=kOutput, calls=%fused_computation.2.clone.1 | convolution fusion | flops 403537920 | bytes 5447685 | tf_op jit(solution)/shard_map/while/body/eval_jaxpr/dot_general | solution.py:28
  63.5 2.6 %fusion.46 = f32[192,2048]{1,0:T(8,128)S(1)} fusion(bf16[512,2048]{1,0:T(8,128)(2,1)} %get-tuple-element.156, f32[4,192,2048]{2,1,0:T(8,128)} %get-tuple-element.155, s32[]{:T(128)} %get-tuple-element.142, f32[2048]{0:T(1024)S(1)} %get-tuple-element.157, bf16[192,512]{1,0:T(8,128)(2,1)S(1)} %get-tuple-element.143, pred[]{:T(512)S(6)} %compare.3), kind=kOutput, calls=%fused_computation.2.clone.1 | convolution fusion | flops 403537920 | bytes 5447685 | tf_op jit(solution)/shard_map/while/body/eval_jaxpr/dot_general | solution.py:28
  66.6 2.6 %fusion.46 = f32[192,2048]{1,0:T(8,128)S(1)} fusion(bf16[512,2048]{1,0:T(8,128)(2,1)} %get-tuple-element.156, f32[4,192,2048]{2,1,0:T(8,128)} %get-tuple-element.155, s32[]{:T(128)} %get-tuple-element.142, f32[2048]{0:T(1024)S(1)} %get-tuple-element.157, bf16[192,512]{1,0:T(8,128)(2,1)S(1)} %get-tuple-element.143, pred[]{:T(512)S(6)} %compare.3), kind=kOutput, calls=%fused_computation.2.clone.1 | convolution fusion | flops 403537920 | bytes 5447685 | tf_op jit(solution)/shard_map/while/body/eval_jaxpr/dot_general | solution.py:28
  69.7 2.6 %fusion.46 = f32[192,2048]{1,0:T(8,128)S(1)} fusion(bf16[512,2048]{1,0:T(8,128)(2,1)} %get-tuple-element.156, f32[4,192,2048]{2,1,0:T(8,128)} %get-tuple-element.155, s32[]{:T(128)} %get-tuple-element.142, f32[2048]{0:T(1024)S(1)} %get-tuple-element.157, bf16[192,512]{1,0:T(8,128)(2,1)S(1)} %get-tuple-element.143, pred[]{:T(512)S(6)} %compare.3), kind=kOutput, calls=%fused_computation.2.clone.1 | convolution fusion | flops 403537920 | bytes 5447685 | tf_op jit(solution)/shard_map/while/body/eval_jaxpr/dot_general | solution.py:28
  72.8 22.6 %all_to_all.24 = bf16[4,192,512]{2,1,0:T(8,128)(2,1)S(1)} all-to-all(bf16[4,192,512]{2,1,0:T(8,128)(2,1)S(1)} %get-tuple-element.42), channel_id=1, replica_groups=mesh['snap'=4,'vert'=8] {'snap'}, dimensions={0} | all-to-all | bytes 1572864 | tf_op jit(solution)/shard_map/all_to_all | solution.py:87
  95.4 0.9 copy.38
  (28 shorter events, 3.1 us)
Async XLA Ops:
  0.0 56.0 %copy-start = (bf16[512,2048]{1,0:T(8,128)(2,1)S(1)}, bf16[512,2048]{1,0:T(8,128)(2,1)}, u32[]{:S(2)}) copy-start(bf16[512,2048]{1,0:T(8,128)(2,1)} %param.19) | copy-start | bytes 6291460
  0.0 11.7 %copy-start.2 = (bf16[1,12,128,128]{3,2,1,0:T(8,128)(2,1)S(1)}, bf16[1,12,128,128]{3,2,1,0:T(8,128)(2,1)}, u32[]{:S(2)}) copy-start(bf16[1,12,128,128]{3,2,1,0:T(8,128)(2,1)} %param.13) | copy-start | bytes 1179652
  0.0 8.6 %collective-permute-start = (bf16[1,768,128]{2,1,0:T(8,128)(2,1)}, bf16[1,768,128]{2,1,0:T(8,128)(2,1)S(1)}, u32[]{:S(2)}, u32[]{:S(2)}) collective-permute-start(bf16[1,768,128]{2,1,0:T(8,128)(2,1)} %param.12), channel_id=1, source_target_pairs={{0,1},{1,2},{2,3},{3,4},{4,5},{5,6},{6,7},{8,9},{9,10},{10,11},{11... | collective-permute-start | bytes 589832 | tf_op jit(solution)/shard_map/ppermute | solution.py:17
  2.1 8.0 %collective-permute-start.1 = (bf16[1,768,128]{2,1,0:T(8,128)(2,1)}, bf16[1,768,128]{2,1,0:T(8,128)(2,1)S(1)}, u32[]{:S(2)}, u32[]{:S(2)}) collective-permute-start(bf16[1,768,128]{2,1,0:T(8,128)(2,1)} %param.12), channel_id=1, source_target_pairs={{1,0},{2,1},{3,2},{4,3},{5,4},{6,5},{7,6},{9,8},{10,9},{11,10},{12... | collective-permute-start | bytes 589832 | tf_op jit(solution)/shard_map/ppermute | solution.py:19
  11.7 3.1 %copy-start.6 = (s32[1,12]{1,0:T(1,128)S(1)}, s32[1,12]{1,0:T(1,128)}, u32[]{:S(2)}) copy-start(s32[1,12]{1,0:T(1,128)} %param.15) | copy-start | bytes 148
  13.1 2.2 %copy-start.4 = (bf16[128,512]{1,0:T(8,128)(2,1)S(1)}, bf16[128,512]{1,0:T(8,128)(2,1)}, u32[]{:S(2)}) copy-start(bf16[128,512]{1,0:T(8,128)(2,1)} %param.17) | copy-start | bytes 393220
  13.1 2.2 %copy-start.5 = (f32[512]{0:T(512)S(1)}, f32[512]{0:T(512)}, u32[]{:S(2)}) copy-start(f32[512]{0:T(512)} %param.18) | copy-start | bytes 6148
  26.4 25.9 %all-to-all-start = ((bf16[4,2,49152]{2,1,0:T(2,128)(2,1)}), bf16[4,2,49152]{2,1,0:T(2,128)(2,1)S(1)}, u32[]{:S(2)}, u32[]{:S(2)}) async-start(bf16[4,2,49152]{2,1,0:T(2,128)(2,1)} %reshape.53), calls=%async_computation | async-start | bytes 1572864 | tf_op jit(solution)/shard_map/all_to_all | solution.py:73
  56.0 4.5 %copy-start.1 = (bf16[4,192,512]{2,1,0:T(8,128)(2,1)S(1)}, bf16[4,192,512]{2,1,0:T(8,128)(2,1)}, u32[]{:S(2)}) copy-start(bf16[4,192,512]{2,1,0:T(8,128)(2,1)} %custom-call.4) | copy-start | bytes 2359300
  56.0 4.5 %copy-start.3 = (f32[2048]{0:T(1024)S(1)}, f32[2048]{0:T(1024)}, u32[]{:S(2)}) copy-start(f32[2048]{0:T(1024)} %param.21) | copy-start | bytes 24580
where the time goes:
time: 96.7 us; the launch traced here: 96.3 us
  blocking collectives  22.6 us (23%)
  waiting for transfers between devices  22.5 us (23%)
  matrix products  17.2 us (18%)
  starting transfers between devices  11.5 us (12%)
  local copies, waits for them, and re-layouts  11.1 us (11%)
  other arithmetic  10.4 us (11%)
    all_to_all x1, blocking collectives, shards(): lax.all_to_all(sequence, 'snap', split_axis=0, concat_axis=1, tiled=True)  22.6 us
    all_to_all x1, waiting for transfers between devices, shards(): lax.all_to_all(conv[None], 'snap', split_axis=1, concat_axis=0, tiled=True)  21 us
    dot_general x4, matrix products, gate_step(): jnp.dot(hidden, w_state, preferred_element_type=jnp.float32)  10.5 us
    unnamed x19, local copies, waits for them, and re-layouts  6.46 us
    unnamed x3, other arithmetic  6.4 us
    all_to_all x1, starting transfers between devices, shards(): lax.all_to_all(conv[None], 'snap', split_axis=1, concat_axis=0, tiled=True)  4.88 us
    ppermute x1, starting transfers between devices, padded(): lax.ppermute(head, axis, [((i + 1) % count, i) for i in range(ends)])  4.54 us
    dot_general x1, matrix products, shards(): jnp.einsum('tvp,pg->tvg', regrouped, w_input, preferred_element_type=jnp....  4.46 us
  transfers between devices with their start and end apart: 3, of which 2 were waited for; matrix products, arithmetic and copies ran while one was open for 1% of the time, Pallas kernels for 0%

commit v1 on v0

--- a/solution.py
+++ b/solution.py
@@ -70,7 +70,10 @@
     conv = jax.nn.relu(jnp.dot(summed, w_conv, preferred_element_type=jnp.float32) + b_conv).astype(
         jnp.bfloat16
     )
-    regrouped = lax.all_to_all(conv[None], "snap", split_axis=1, concat_axis=0, tiled=True)
+    block = conv[None]
+    pieces = jnp.split(block, lax.axis_size("snap"), axis=1)
+    received = lax.all_to_all(jnp.stack(pieces), "snap", 0, 0)
+    regrouped = jnp.concatenate(received, axis=0)
     pre_all = jnp.einsum("tvp,pg->tvg", regrouped, w_input, preferred_element_type=jnp.float32)
     slice_rows = regrouped.shape[1]
 

time: 96.7 us -> 87 us (0.90)
  local copies, waits for them, and re-layouts: 11.1 us -> 3.27 us
  other arithmetic: 10.4 us -> 7.72 us
  blocking collectives: 22.6 us -> 23.6 us
    unnamed x3 -> x2, other arithmetic: 6.4 us -> 0.01 us
    unnamed x19 -> x13, local copies, waits for them, and re-layouts: 6.46 us -> 0.9 us
    dynamic_update_slice x4, other arithmetic: 1.71 us -> 4.42 us  [shards(): _, sequence = lax.scan(advance, start_state, pre_all)]
    broadcast_in_dim x1 -> x0, local copies, waits for them, and re-layouts: 2.37 us -> none  [shards(): conv[None]]
    all_to_all x1, blocking collectives: 22.6 us -> 23.6 us  [shards(): lax.all_to_all(sequence, 'snap', split_axis=0, concat_axis=1, tiled=True)]
    another operation x0 -> x1, other arithmetic: none -> 0.99 us  [shards(): received = lax.all_to_all(jnp.stack(pieces), 'snap', 0, 0)]
  transfers between devices with their start and end apart: 3 -> 3, of which waited for: 2 -> 2; matrix products, arithmetic and copies ran while one was open for 1% -> 2% of each run, Pallas kernels for 0% -> 0%
where the time goes in v1:
time: 87 us; the launch traced here: 86.6 us
  blocking collectives  23.6 us (27%)
  waiting for transfers between devices  22.5 us (26%)
  matrix products  17.2 us (20%)
  starting transfers between devices  11.5 us (13%)
  other arithmetic  7.72 us (9%)
  local copies, waits for them, and re-layouts  3.27 us (4%)
    all_to_all x1, blocking collectives, shards(): lax.all_to_all(sequence, 'snap', split_axis=0, concat_axis=1, tiled=True)  23.6 us
    all_to_all x1, waiting for transfers between devices, shards(): received = lax.all_to_all(jnp.stack(pieces), 'snap', 0, 0)  21 us
    dot_general x4, matrix products, gate_step(): jnp.dot(hidden, w_state, preferred_element_type=jnp.float32)  10.5 us
    all_to_all x1, starting transfers between devices, shards(): received = lax.all_to_all(jnp.stack(pieces), 'snap', 0, 0)  4.88 us
    ppermute x1, starting transfers between devices, padded(): lax.ppermute(head, axis, [((i + 1) % count, i) for i in range(ends)])  4.54 us
    dot_general x1, matrix products, shards(): jnp.einsum('tvp,pg->tvg', regrouped, w_input, preferred_element_type=jnp....  4.45 us
    dynamic_update_slice x4, other arithmetic, shards(): _, sequence = lax.scan(advance, start_state, pre_all)  4.42 us
    ppermute x1, starting transfers between devices, padded(): lax.ppermute(tail, axis, [(i, (i + 1) % count) for i in range(ends)])  2.04 us
  transfers between devices with their start and end apart: 3, of which 2 were waited for; matrix products, arithmetic and copies ran while one was open for 2% of the time, Pallas kernels for 0%

profile of v1, /device:TPU:4, one launch (start us, length us, event | category | flops | bytes accessed | tf_op | source)
XLA Modules:
  0.0 86.6 jit_solution(13449764888046697329)
XLA Ops:
  0.0 2.0 %collective-permute-start = (bf16[1,768,128]{2,1,0:T(8,128)(2,1)}, bf16[1,768,128]{2,1,0:T(8,128)(2,1)S(1)}, u32[]{:S(2)}, u32[]{:S(2)}) collective-permute-start(bf16[1,768,128]{2,1,0:T(8,128)(2,1)} %param.12), channel_id=1, source_target_pairs={{0,1},{1,2},{2,3},{3,4},{4,5},{5,6},{6,7},{8,9},{9,10},{10,11},{11... | collective-permute-start | bytes 589832 | tf_op jit(solution)/shard_map/ppermute | solution.py:17
  2.1 4.5 %collective-permute-start.1 = (bf16[1,768,128]{2,1,0:T(8,128)(2,1)}, bf16[1,768,128]{2,1,0:T(8,128)(2,1)S(1)}, u32[]{:S(2)}, u32[]{:S(2)}) collective-permute-start(bf16[1,768,128]{2,1,0:T(8,128)(2,1)} %param.12), channel_id=1, source_target_pairs={{1,0},{2,1},{3,2},{4,3},{5,4},{6,5},{7,6},{9,8},{10,9},{11,10},{12... | collective-permute-start | bytes 589832 | tf_op jit(solution)/shard_map/ppermute | solution.py:19
  6.6 0.7 fusion.35
  7.9 0.7 compare_and_fusion
  8.6 1.5 %collective-permute-done.1 = bf16[1,768,128]{2,1,0:T(8,128)(2,1)S(1)} collective-permute-done((bf16[1,768,128]{2,1,0:T(8,128)(2,1)}, bf16[1,768,128]{2,1,0:T(8,128)(2,1)S(1)}, u32[]{:S(2)}, u32[]{:S(2)}) %collective-permute-start.1) | collective-permute-done | bytes 196640 | tf_op jit(solution)/shard_map/ppermute | solution.py:19
  10.1 1.0 %pad_maximum_fusion.1 = bf16[1,2304,128]{2,1,0:T(8,128)(2,1)S(1)} fusion(bf16[1,768,128]{2,1,0:T(8,128)(2,1)S(1)} %collective-permute-done.1, bf16[1,768,128]{2,1,0:T(8,128)(2,1)} %param.12, bf16[1,768,128]{2,1,0:T(8,128)(2,1)S(1)} %collective-permute-done), kind=kLoop, calls=%fused_computation.35 | loop fusion | flops 1769472 | bytes 1179648 | tf_op jit(solution)/shard_map/concatenate | solution.py:15
  11.1 0.6 gather_fusion
  11.7 1.4 %fusion.25 = f32[12,128,128]{2,1,0:T(8,128)} fusion(bf16[1,12,128,128]{3,2,1,0:T(8,128)(2,1)S(1)} %copy-done.1, bf16[12,128,128]{2,1,0:T(8,128)(2,1)S(1)} %gather_fusion, pred[12]{0:T(512)(128)(4,1)S(1)} %compare_and_fusion), kind=kOutput, calls=%fused_computation.36 | convolution fusion | flops 50528256 | bytes 1572876 | tf_op jit(solution)/shard_map/ebk,ekf->ebf/dot_general | solution.py:61
  13.1 1.7 %copy.12 = f32[12,128,128]{1,0,2:T(8,128)S(1)} copy(f32[12,128,128]{2,1,0:T(8,128)} %fusion.25) | data formatting | bytes 1572864 | tf_op jit(solution)/shard_map/ebk,ekf->ebf/dot_general | solution.py:61
  15.8 1.0 %pad_maximum_fusion = bf16[4,1,192,512]{3,2,1,0:T(8,128)(2,1)} fusion(bf16[1,1,192,512]{3,2,1,0:T(8,128)(2,1)S(1)} %get-tuple-element.85, bf16[1,1,192,512]{3,2,1,0:T(8,128)(2,1)S(1)} %get-tuple-element.86, bf16[1,1,192,512]{3,2,1,0:T(8,128)(2,1)S(1)} %get-tuple-element.87, bf16[1,1,192,512]{3,2,1,0:T(8,128)(2,1)S(1)} %get-tuple-element.84), kind=kLoop, calls=%fused_computation.33 | loop fusion | flops 1179648 | bytes 1572864 | tf_op jit(solution)/shard_map/stack | solution.py:75
  16.8 4.9 %all-to-all-start = ((bf16[4,1,192,512]{3,2,1,0:T(8,128)(2,1)}), bf16[4,1,192,512]{3,2,1,0:T(8,128)(2,1)S(1)}, u32[]{:S(2)}, u32[]{:S(2)}) async-start(bf16[4,1,192,512]{3,2,1,0:T(8,128)(2,1)} %pad_maximum_fusion), calls=%async_computation | async-start | bytes 1572864 | tf_op jit(solution)/shard_map/all_to_all | solution.py:75
  21.7 21.0 %all-to-all-done = bf16[4,1,192,512]{3,2,1,0:T(8,128)(2,1)S(1)} async-done(((bf16[4,1,192,512]{3,2,1,0:T(8,128)(2,1)}), bf16[4,1,192,512]{3,2,1,0:T(8,128)(2,1)S(1)}, u32[]{:S(2)}, u32[]{:S(2)}) %all-to-all-start) | async-done | bytes 786464 | tf_op jit(solution)/shard_map/all_to_all | solution.py:75
  42.7 4.4 %fusion.20 = f32[4,192,2048]{2,1,0:T(8,128)} fusion(bf16[512,2048]{1,0:T(8,128)(2,1)S(1)} %copy-done, bf16[4,1,192,512]{3,2,1,0:T(8,128)(2,1)S(1)} %all-to-all-done), kind=kOutput, calls=%fused_computation.27 | convolution fusion | flops 1610612736 | bytes 9175040 | tf_op jit(solution)/shard_map/tvp,pg->tvg/dot_general | solution.py:77
  47.1 15.0 %while.15 = (s32[]{:T(128)}, bf16[192,512]{1,0:T(8,128)(2,1)S(1)}, f32[192,512]{1,0:T(8,128)S(1)}, bf16[4,192,512]{2,1,0:T(8,128)(2,1)}, f32[4,192,2048]{2,1,0:T...) while((s32[]{:T(128)}, bf16[192,512]{1,0:T(8,128)(2,1)S(1)}, ...), condition=%wide.region_1.2_spmd.clone, body=%wide.region_0.1_spmd.clone.sunk | while | flops 405110784 | bytes 8200812 | solution.py:89
  47.1 2.6 %fusion.47 = f32[192,2048]{1,0:T(8,128)S(1)} fusion(bf16[512,2048]{1,0:T(8,128)(2,1)} %get-tuple-element.160, f32[4,192,2048]{2,1,0:T(8,128)} %get-tuple-element.159, s32[]{:T(128)} %get-tuple-element.146, f32[2048]{0:T(1024)S(1)} %get-tuple-element.161, bf16[192,512]{1,0:T(8,128)(2,1)S(1)} %get-tuple-element.147, pred[]{:T(512)S(6)} %compare.3), kind=kOutput, calls=%fused_computation.2.clone.1 | convolution fusion | flops 403537920 | bytes 5447685 | tf_op jit(solution)/shard_map/while/body/eval_jaxpr/dot_general | solution.py:28
  49.8 1.1 %bitcast_dynamic-update-slice_fusion.2 = (bf16[4,192,512]{2,1,0:T(8,128)(2,1)}, bf16[192,512]{1,0:T(8,128)(2,1)S(1)}, f32[192,512]{1,0:T(8,128)S(1)}) fusion(bf16[4,192,512]{2,1,0:T(8,128)(2,1)} %get-tuple-element.149, s32[]{:T(128)} %get-tuple-element.146, f32[192,2048]{1,0:T(8,128)S(1)} %fusion.47, f32[192,512]{1,0:T(8,128)S(1)} %get-tuple-element.148, ...), kind=kLoop, calls=%fused_computation.22.clone.1 | loop fusion | flops 1572864 | bytes 2753025 | tf_op jit(solution)/shard_map/while/body/jit(dynamic_update_index_in_dim)/dynamic_update_slice | solution.py:89
  50.9 2.6 %fusion.47 = f32[192,2048]{1,0:T(8,128)S(1)} fusion(bf16[512,2048]{1,0:T(8,128)(2,1)} %get-tuple-element.160, f32[4,192,2048]{2,1,0:T(8,128)} %get-tuple-element.159, s32[]{:T(128)} %get-tuple-element.146, f32[2048]{0:T(1024)S(1)} %get-tuple-element.161, bf16[192,512]{1,0:T(8,128)(2,1)S(1)} %get-tuple-element.147, pred[]{:T(512)S(6)} %compare.3), kind=kOutput, calls=%fused_computation.2.clone.1 | convolution fusion | flops 403537920 | bytes 5447685 | tf_op jit(solution)/shard_map/while/body/eval_jaxpr/dot_general | solution.py:28
  53.5 1.1 %bitcast_dynamic-update-slice_fusion.2 = (bf16[4,192,512]{2,1,0:T(8,128)(2,1)}, bf16[192,512]{1,0:T(8,128)(2,1)S(1)}, f32[192,512]{1,0:T(8,128)S(1)}) fusion(bf16[4,192,512]{2,1,0:T(8,128)(2,1)} %get-tuple-element.149, s32[]{:T(128)} %get-tuple-element.146, f32[192,2048]{1,0:T(8,128)S(1)} %fusion.47, f32[192,512]{1,0:T(8,128)S(1)} %get-tuple-element.148, ...), kind=kLoop, calls=%fused_computation.22.clone.1 | loop fusion | flops 1572864 | bytes 2753025 | tf_op jit(solution)/shard_map/while/body/jit(dynamic_update_index_in_dim)/dynamic_update_slice | solution.py:89
  54.6 2.6 %fusion.47 = f32[192,2048]{1,0:T(8,128)S(1)} fusion(bf16[512,2048]{1,0:T(8,128)(2,1)} %get-tuple-element.160, f32[4,192,2048]{2,1,0:T(8,128)} %get-tuple-element.159, s32[]{:T(128)} %get-tuple-element.146, f32[2048]{0:T(1024)S(1)} %get-tuple-element.161, bf16[192,512]{1,0:T(8,128)(2,1)S(1)} %get-tuple-element.147, pred[]{:T(512)S(6)} %compare.3), kind=kOutput, calls=%fused_computation.2.clone.1 | convolution fusion | flops 403537920 | bytes 5447685 | tf_op jit(solution)/shard_map/while/body/eval_jaxpr/dot_general | solution.py:28
  57.3 1.1 %bitcast_dynamic-update-slice_fusion.2 = (bf16[4,192,512]{2,1,0:T(8,128)(2,1)}, bf16[192,512]{1,0:T(8,128)(2,1)S(1)}, f32[192,512]{1,0:T(8,128)S(1)}) fusion(bf16[4,192,512]{2,1,0:T(8,128)(2,1)} %get-tuple-element.149, s32[]{:T(128)} %get-tuple-element.146, f32[192,2048]{1,0:T(8,128)S(1)} %fusion.47, f32[192,512]{1,0:T(8,128)S(1)} %get-tuple-element.148, ...), kind=kLoop, calls=%fused_computation.22.clone.1 | loop fusion | flops 1572864 | bytes 2753025 | tf_op jit(solution)/shard_map/while/body/jit(dynamic_update_index_in_dim)/dynamic_update_slice | solution.py:89
  58.4 2.6 %fusion.47 = f32[192,2048]{1,0:T(8,128)S(1)} fusion(bf16[512,2048]{1,0:T(8,128)(2,1)} %get-tuple-element.160, f32[4,192,2048]{2,1,0:T(8,128)} %get-tuple-element.159, s32[]{:T(128)} %get-tuple-element.146, f32[2048]{0:T(1024)S(1)} %get-tuple-element.161, bf16[192,512]{1,0:T(8,128)(2,1)S(1)} %get-tuple-element.147, pred[]{:T(512)S(6)} %compare.3), kind=kOutput, calls=%fused_computation.2.clone.1 | convolution fusion | flops 403537920 | bytes 5447685 | tf_op jit(solution)/shard_map/while/body/eval_jaxpr/dot_general | solution.py:28
  61.0 1.1 %bitcast_dynamic-update-slice_fusion.2 = (bf16[4,192,512]{2,1,0:T(8,128)(2,1)}, bf16[192,512]{1,0:T(8,128)(2,1)S(1)}, f32[192,512]{1,0:T(8,128)S(1)}) fusion(bf16[4,192,512]{2,1,0:T(8,128)(2,1)} %get-tuple-element.149, s32[]{:T(128)} %get-tuple-element.146, f32[192,2048]{1,0:T(8,128)S(1)} %fusion.47, f32[192,512]{1,0:T(8,128)S(1)} %get-tuple-element.148, ...), kind=kLoop, calls=%fused_computation.22.clone.1 | loop fusion | flops 1572864 | bytes 2753025 | tf_op jit(solution)/shard_map/while/body/jit(dynamic_update_index_in_dim)/dynamic_update_slice | solution.py:89
  62.1 23.6 %all_to_all.17 = bf16[4,192,512]{2,1,0:T(8,128)(2,1)S(1)} all-to-all(bf16[4,192,512]{2,1,0:T(8,128)(2,1)} %get-tuple-element.42), channel_id=1, replica_groups=mesh['snap'=4,'vert'=8] {'snap'}, dimensions={0} | all-to-all | bytes 1572864 | tf_op jit(solution)/shard_map/all_to_all | solution.py:90
  85.7 0.9 %copy.28 = bf16[1,768,512]{2,1,0:T(8,128)(2,1)} copy(bf16[1,768,512]{2,1,0:T(8,128)(2,1)S(1)} %bitcast.50) | data formatting | bytes 1572864
  (22 shorter events, 1.0 us)
Async XLA Ops:
  0.0 42.7 %copy-start = (bf16[512,2048]{1,0:T(8,128)(2,1)S(1)}, bf16[512,2048]{1,0:T(8,128)(2,1)}, u32[]{:S(2)}) copy-start(bf16[512,2048]{1,0:T(8,128)(2,1)} %param.19) | copy-start | bytes 6291460
  0.0 11.7 %copy-start.1 = (bf16[1,12,128,128]{3,2,1,0:T(8,128)(2,1)S(1)}, bf16[1,12,128,128]{3,2,1,0:T(8,128)(2,1)}, u32[]{:S(2)}) copy-start(bf16[1,12,128,128]{3,2,1,0:T(8,128)(2,1)} %param.13) | copy-start | bytes 1179652
  0.0 8.6 %collective-permute-start = (bf16[1,768,128]{2,1,0:T(8,128)(2,1)}, bf16[1,768,128]{2,1,0:T(8,128)(2,1)S(1)}, u32[]{:S(2)}, u32[]{:S(2)}) collective-permute-start(bf16[1,768,128]{2,1,0:T(8,128)(2,1)} %param.12), channel_id=1, source_target_pairs={{0,1},{1,2},{2,3},{3,4},{4,5},{5,6},{6,7},{8,9},{9,10},{10,11},{11... | collective-permute-start | bytes 589832 | tf_op jit(solution)/shard_map/ppermute | solution.py:17
  2.1 8.0 %collective-permute-start.1 = (bf16[1,768,128]{2,1,0:T(8,128)(2,1)}, bf16[1,768,128]{2,1,0:T(8,128)(2,1)S(1)}, u32[]{:S(2)}, u32[]{:S(2)}) collective-permute-start(bf16[1,768,128]{2,1,0:T(8,128)(2,1)} %param.12), channel_id=1, source_target_pairs={{1,0},{2,1},{3,2},{4,3},{5,4},{6,5},{7,6},{9,8},{10,9},{11,10},{12... | collective-permute-start | bytes 589832 | tf_op jit(solution)/shard_map/ppermute | solution.py:19
  11.7 3.1 %copy-start.5 = (s32[1,12]{1,0:T(1,128)S(1)}, s32[1,12]{1,0:T(1,128)}, u32[]{:S(2)}) copy-start(s32[1,12]{1,0:T(1,128)} %param.15) | copy-start | bytes 148
  13.1 2.2 %copy-start.3 = (bf16[128,512]{1,0:T(8,128)(2,1)S(1)}, bf16[128,512]{1,0:T(8,128)(2,1)}, u32[]{:S(2)}) copy-start(bf16[128,512]{1,0:T(8,128)(2,1)} %param.17) | copy-start | bytes 393220
  13.1 2.2 %copy-start.4 = (f32[512]{0:T(512)S(1)}, f32[512]{0:T(512)}, u32[]{:S(2)}) copy-start(f32[512]{0:T(512)} %param.18) | copy-start | bytes 6148
  16.8 25.9 %all-to-all-start = ((bf16[4,1,192,512]{3,2,1,0:T(8,128)(2,1)}), bf16[4,1,192,512]{3,2,1,0:T(8,128)(2,1)S(1)}, u32[]{:S(2)}, u32[]{:S(2)}) async-start(bf16[4,1,192,512]{3,2,1,0:T(8,128)(2,1)} %pad_maximum_fusion), calls=%async_computation | async-start | bytes 1572864 | tf_op jit(solution)/shard_map/all_to_all | solution.py:75
  21.7 25.5 %copy-start.2 = (f32[2048]{0:T(1024)S(1)}, f32[2048]{0:T(1024)}, u32[]{:S(2)}) copy-start(f32[2048]{0:T(1024)} %param.21) | copy-start | bytes 24580
